TPU v7x, 256 devices: a whole 4x4x8 slice. The times are simulated.
256 devices in a mesh: events: 8 (over x, z_lo), shells: 32 (over y, z_hi, core).
Axes of the slice: x: 4, y: 4, z: 8 (z_hi: 4, z_lo: 2; z = z_hi * 2 + z_lo), core: 2. Of those that a mesh axis runs over, the one named last changes fastest.
Arguments:
- model: bfloat16 [2097152], P('shells'), may hold values from -6 to 6
- sensitivity: bfloat16 [131072, 64, 128], P(('events', 'shells')), may hold values from -0.1875 to 0.1875
- pick_block: int32 [131072], P(('events', 'shells')), may hold values from 0 to 2047, as said below
- cell_block: int32 [131072], P(('events', 'shells')), may hold values from 0 to 511
- blk_count: int32 [256], P(('events', 'shells')), may hold values from 128 to 512, as said below
- observed: float32 [1048576], P(('events', 'shells')), may hold values from -6 to 6
- pick_weight: float32 [1048576], P(('events', 'shells')), may hold values from 0.2 to 15
- station: int32 [1048576], P(('events', 'shells')), may hold values from 0 to 2047
Outputs:
- gradient: float32 [2097152], P('shells')
- correction: float32 [2048], replicated
- weighted: float32 [1048576], P(('events', 'shells'))
Inputs may be any that keep to these rules, and one draw needn't show every extreme that they name: `blk_count`: each device uses its first slots; some device uses all 512 in every draw. The owner of a slot is pick_block // 64. Among the used slots of one device, at most 32 have one owner; in every event group some owner gets exactly 32 from every device of the group.
All inputs are finite; a program needn't handle non-finite values.
Results may differ from a plain program's by a relative error of at most 0.0026.
Values may be sent and summed in bfloat16 or wider, within the bound.
No kernel may reach another device: no remote copies, remote signals or barrier semaphores. Data moves between devices by JAX's collectives and lax.ppermute only.
A program may use at most 64 MiB of HBM per device.

v0:
```python
import jax
import jax.numpy as jnp
from jax import lax
from jax.sharding import PartitionSpec as P

PICK_BLK = 64
CELL_BLK = 128
STATIONS = 2048


def local(model, sensitivity, pick_block, cell_block, blk_count, observed, pick_weight, station):
    slot_count = blk_count[0]
    slot_total = sensitivity.shape[0]
    slot_step = min(32, slot_total)
    model_rows = model.reshape(-1, CELL_BLK)
    owned_picks = observed.shape[0]
    owned_blocks = owned_picks // PICK_BLK
    shell_count = lax.axis_size("shells")
    group_rows = owned_blocks * shell_count
    turns = (slot_count + slot_step - 1) // slot_step

    def slot_range(turn):
        offset = turn * slot_step
        blocks = lax.dynamic_slice_in_dim(sensitivity, offset, slot_step, 0)
        picks_of = lax.dynamic_slice_in_dim(pick_block, offset, slot_step, 0)
        cells_of = lax.dynamic_slice_in_dim(cell_block, offset, slot_step, 0)
        alive = offset + jnp.arange(slot_step, dtype=jnp.int32) < slot_count
        return (blocks, picks_of, cells_of, alive)

    def slot_values(turn):
        blocks, picks_of, cells_of, alive = slot_range(turn)
        values = jnp.einsum(
            "kpc,kc->kp", blocks, model_rows[cells_of], preferred_element_type=jnp.float32
        )
        return (jnp.where(alive[:, None], values, 0.0), picks_of)

    def forward_turn(turn, partials):
        values, picks_of = slot_values(turn)
        return partials.at[picks_of].add(values)

    partials = lax.fori_loop(0, turns, forward_turn, jnp.zeros((group_rows, PICK_BLK), jnp.float32))
    flat_terms = partials.reshape(-1)
    summed = lax.psum(flat_terms, "shells")
    predicted = lax.dynamic_slice_in_dim(
        summed, lax.axis_index("shells") * owned_picks, owned_picks, 0
    )
    misfit = observed - predicted
    numer_local = jax.ops.segment_sum(pick_weight * misfit, station, num_segments=STATIONS)
    denom_local = jax.ops.segment_sum(pick_weight, station, num_segments=STATIONS)
    numer, denom = lax.psum((numer_local, denom_local), ("events", "shells"))
    correction = numer / (denom + 1.0)
    weighted = pick_weight * (misfit - correction[station])
    weighted_half = weighted.astype(jnp.bfloat16)
    group_resid = lax.all_gather(weighted_half, "shells", axis=0, tiled=True).reshape(
        group_rows, PICK_BLK
    )

    def backward_turn(turn, grads):
        blocks, picks_of, cells_of, alive = slot_range(turn)
        terms = jnp.einsum(
            "kpc,kp->kc", blocks, group_resid[picks_of], preferred_element_type=jnp.float32
        )
        terms = jnp.where(alive[:, None], terms, 0.0)
        return grads.at[cells_of].add(terms)

    grads = lax.fori_loop(0, turns, backward_turn, jnp.zeros(model_rows.shape, jnp.float32))
    gradient = lax.psum(grads.reshape(-1), "events")
    return (gradient, correction, weighted)


def solution(mesh):
    placed = (
        P("shells"),
        P(("events", "shells"), None, None),
        P(("events", "shells")),
        P(("events", "shells")),
        P(("events", "shells")),
        P(("events", "shells")),
        P(("events", "shells")),
        P(("events", "shells")),
    )
    return jax.shard_map(
        local,
        mesh=mesh,
        in_specs=placed,
        out_specs=(P("shells"), P(), P(("events", "shells"))),
        check_vma=False,
    )
```

profile of v0, /device:TPU:8, one launch (start us, length us, event | category | flops | bytes accessed | tf_op | source)
XLA Modules:
  0.0 702.0 jit_solution(82583176409720336)
XLA Ops:
  8.0 44.9 %while.20 = (s32[]{:T(128)}, f32[2048,64]{1,0:T(8,128)S(1)}, s32[]{:T(128)}, s32[512]{0:T(512)}, s32[]{:T(128)}, /*index=5*/bf16[512,64,128]{2,1,0:T(8,128)(2,1)...) while((s32[]{:T(128)}, f32[2048,64]{1,0:T(8,128)S(1)}, ...), condition=%wide.region_2.3_spmd, body=%wide.region_0.2_spmd.sunk | while | flops 529670 | bytes 1103327 | solution.py:41
  8.8 1.5 gather_fusion
  10.3 1.4 fusion.34
  14.4 1.5 gather_fusion
  15.9 1.4 fusion.34
  20.0 1.5 gather_fusion
  21.5 1.4 fusion.34
  25.6 1.5 gather_fusion
  27.1 1.4 fusion.34
  31.3 1.5 gather_fusion
  32.8 1.4 fusion.34
  36.9 1.5 gather_fusion
  38.4 1.4 fusion.34
  42.5 1.5 gather_fusion
  44.0 1.4 fusion.34
  48.1 1.5 gather_fusion
  49.6 1.4 fusion.34
  54.0 22.1 %scatter_custom_fusion.3 = f32[2048]{0:T(1024)S(1)} fusion(s32[4096]{0:T(1024)S(1)} %copy-done.4, f32[4096]{0:T(1024)S(1)} %copy-done.2, f32[]{:T(128)} %constant.36.clone.1), kind=kCustom, calls=%fused_computation.37 | custom fusion | flops 4096 | bytes 8196 | tf_op jit(solution)/shard_map/scatter-add | solution.py:49
  76.1 299.0 %all-reduce.4.cloned.1.call-done = f32[131072]{0:T(1024)} async-done(((f32[131072]{0:T(1024)}), f32[131072]{0:T(1024)}) %all-reduce.4.cloned.1.call-update) | async-done | bytes 524304 | tf_op jit(solution)/shard_map/psum | solution.py:43
  375.9 22.1 %scatter_custom_fusion.2 = f32[2048]{0:T(1024)S(1)} fusion(s32[4096]{0:T(1024)S(1)} %copy-done.4, f32[4096]{0:T(1024)S(1)} %fusion.17, f32[]{:T(128)} %constant.36.clone.1), kind=kCustom, calls=%fused_computation.39 | custom fusion | flops 4096 | bytes 8196 | tf_op jit(solution)/shard_map/scatter-add | solution.py:48
  398.0 88.2 %all-reduce = (f32[2048]{0:T(1024)S(1)}, f32[2048]{0:T(1024)S(1)}) all-reduce(f32[2048]{0:T(1024)S(1)} %scatter_custom_fusion.2, f32[2048]{0:T(1024)S(1)} %scatter_custom_fusion.3), channel_id=1, replica_groups=mesh['events'=8,'shells'=32] {'events','shells'}, use_global_device_ids=true, to_apply=%region_5.6 | all-reduce | flops 4096 | bytes 32768 | tf_op jit(solution)/shard_map/psum | solution.py:50
  486.2 23.0 %gather_fusion.2 = f32[4096]{0:T(1024)S(1)} fusion(f32[2048]{0:T(1024)S(1)} %add_divide_fusion, s32[4096]{0:T(1024)S(1)} %fusion.16), kind=kCustom, calls=%fused_computation.2 | custom fusion | bytes 49152 | tf_op jit(solution)/shard_map/gather | solution.py:52
  509.2 1.3 fusion.22
  510.6 37.3 %all_gather.3 = bf16[131072]{0:T(1024)(128)(2,1)S(1)} all-gather(bf16[4096]{0:T(1024)(128)(2,1)S(1)} %get-tuple-element.125), channel_id=1, replica_groups=mesh['events'=8,'shells'=32] {'shells'}, dimensions={0}, use_global_device_ids=true | all-gather | bytes 270336 | tf_op jit(solution)/shard_map/all_gather | solution.py:54
  548.1 34.4 %while.21 = (s32[]{:T(128)}, f32[512,128]{1,0:T(8,128)S(1)}, s32[]{:T(128)}, s32[512]{0:T(512)}, s32[]{:T(128)}, /*index=5*/bf16[512,64,128]{2,1,0:T(8,128)(2,1)...) while((s32[]{:T(128)}, f32[512,128]{1,0:T(8,128)S(1)}, ...), condition=%wide.region_10.11_spmd, body=%wide.region_8.10_spmd.sunk | while | flops 533766 | bytes 837087 | solution.py:66
  549.5 1.3 fusion.38
  562.4 1.3 fusion.38
  566.7 1.3 fusion.38
  571.0 1.3 fusion.38
  575.3 1.3 fusion.38
  583.2 110.4 %all-reduce.6.cloned.1.call-done = f32[65536]{0:T(1024)} async-done(((f32[65536]{0:T(1024)}), f32[65536]{0:T(1024)}) %all-reduce.6.cloned.1.call-update) | async-done | bytes 262160 | tf_op jit(solution)/shard_map/psum | solution.py:67
  693.5 1.7 copy.40
  (96 shorter events, 51.9 us)
Async XLA Ops:
  7.2 46.8 %copy-start.2 = (f32[4096]{0:T(1024)S(1)}, f32[4096]{0:T(1024)}, u32[]{:S(2)}) copy-start(f32[4096]{0:T(1024)} %param.18) | copy-start | bytes 49156
  7.2 46.8 %copy-start.4 = (s32[4096]{0:T(1024)S(1)}, s32[4096]{0:T(1024)}, u32[]{:S(2)}) copy-start(s32[4096]{0:T(1024)} %param.19) | copy-start | bytes 49156
  7.2 368.0 %copy-start.3 = (f32[4096]{0:T(1024)S(1)}, f32[4096]{0:T(1024)}, u32[]{:S(2)}) copy-start(f32[4096]{0:T(1024)} %param.17) | copy-start | bytes 49156
  7.2 368.0 %all-reduce.4.cloned.1.call-start = ((), (), s32[]{:S(2)}) async-start(), calls=%async_computation | async-start | bytes 1048576 | tf_op jit(solution)/shard_map/psum | solution.py:43
  54.0 639.6 %all-reduce.6.cloned.1.call-start = ((), (), s32[]{:S(2)}) async-start(), calls=%async_computation.1 | async-start | bytes 524288 | tf_op jit(solution)/shard_map/psum | solution.py:67
  486.2 23.0 %copy-start = (f32[2048]{0:T(1024)}, f32[2048]{0:T(1024)S(1)}, u32[]{:S(2)}) copy-start(f32[2048]{0:T(1024)S(1)} %add_divide_fusion) | copy-start | bytes 24580
  582.4 0.7 copy-start.1
Sparse Core Ops, SparseCore 0:
  54.1 321.0 all-reduce.3
  583.3 110.1 all-reduce.5
where the time goes:
time: 705 us; the launch traced here: 702 us
  waiting for transfers between devices  409 us (58%)
  blocking collectives  125 us (18%)
  other arithmetic  86.6 us (12%)
  local copies, waits for them, and re-layouts  43.5 us (6%)
  matrix products  21.4 us (3%)
  between operations  14.8 us (2%)
    psum x1, waiting for transfers between devices, local(): summed = lax.psum(flat_terms, 'shells')  299 us
    psum x1, waiting for transfers between devices, local(): gradient = lax.psum(grads.reshape(-1), 'events')  110 us
    psum x1, blocking collectives, local(): numer, denom = lax.psum((numer_local, denom_local), ('events', 'shells'))  88.2 us
    all_gather x1, blocking collectives, local(): lax.all_gather(weighted_half, 'shells', axis=0, tiled=True)  37.3 us
    gather x1, local copies, waits for them, and re-layouts, local(): weighted = pick_weight * (misfit - correction[station])  23 us
    scatter-add x1, other arithmetic, local(): jax.ops.segment_sum(pick_weight, station, num_segments=STATIONS)  22.1 us
    scatter-add x1, other arithmetic, local(): jax.ops.segment_sum(pick_weight * misfit, station, num_segments=STATIONS)  22.1 us
  transfers between devices with their start and end apart: 2, of which 2 were waited for; matrix products, arithmetic and copies ran while one was open for 3% of the time, Pallas kernels for 0%

commit v1 on v0

--- a/solution.py
+++ b/solution.py
@@ -64,7 +64,7 @@
         return grads.at[cells_of].add(terms)
 
     grads = lax.fori_loop(0, turns, backward_turn, jnp.zeros(model_rows.shape, jnp.float32))
-    gradient = lax.psum(grads.reshape(-1), "events")
+    gradient = jnp.sum(lax.all_gather(grads.reshape(-1), "events"), axis=0)
     return (gradient, correction, weighted)
 
 

time: 705 us -> 683 us (0.969)
  waiting for transfers between devices: 409 us -> 385 us
    psum x1 -> x0, waiting for transfers between devices: 110 us -> none  [local(): gradient = lax.psum(grads.reshape(-1), 'events')]
    all_gather x0 -> x1, waiting for transfers between devices: none -> 86.1 us  [local(): gradient = jnp.sum(lax.all_gather(grads.reshape(-1), 'events'), axis=0)]
where the time goes in v1:
time: 683 us; the launch traced here: 680 us
  waiting for transfers between devices  385 us (56%)
  blocking collectives  125 us (18%)
  other arithmetic  90.4 us (13%)
  local copies, waits for them, and re-layouts  41.9 us (6%)
  matrix products  21.4 us (3%)
  between operations  14.8 us (2%)
    psum x1, waiting for transfers between devices, local(): summed = lax.psum(flat_terms, 'shells')  299 us
    psum x1, blocking collectives, local(): numer, denom = lax.psum((numer_local, denom_local), ('events', 'shells'))  88.2 us
    all_gather x1, waiting for transfers between devices, local(): gradient = jnp.sum(lax.all_gather(grads.reshape(-1), 'events'), axis=0)  86.1 us
    all_gather x1, blocking collectives, local(): lax.all_gather(weighted_half, 'shells', axis=0, tiled=True)  37.3 us
    gather x1, local copies, waits for them, and re-layouts, local(): weighted = pick_weight * (misfit - correction[station])  23 us
    scatter-add x1, other arithmetic, local(): jax.ops.segment_sum(pick_weight, station, num_segments=STATIONS)  22.1 us
    scatter-add x1, other arithmetic, local(): jax.ops.segment_sum(pick_weight * misfit, station, num_segments=STATIONS)  22.1 us
  transfers between devices with their start and end apart: 2, of which 2 were waited for; matrix products, arithmetic and copies ran while one was open for 3% of the time, Pallas kernels for 0%

profile of v1, /device:TPU:8, one launch (start us, length us, event | category | flops | bytes accessed | tf_op | source)
XLA Modules:
  0.0 679.9 jit_solution(4348226451509024863)
XLA Ops:
  8.0 44.9 %while.20 = (s32[]{:T(128)}, f32[2048,64]{1,0:T(8,128)S(1)}, s32[]{:T(128)}, s32[512]{0:T(512)}, s32[]{:T(128)}, /*index=5*/bf16[512,64,128]{2,1,0:T(8,128)(2,1)...) while((s32[]{:T(128)}, f32[2048,64]{1,0:T(8,128)S(1)}, ...), condition=%wide.region_2.3_spmd, body=%wide.region_0.2_spmd.sunk | while | flops 529670 | bytes 1103327 | solution.py:41
  8.8 1.5 gather_fusion
  10.3 1.4 fusion.34
  14.4 1.5 gather_fusion
  15.9 1.4 fusion.34
  20.0 1.5 gather_fusion
  21.5 1.4 fusion.34
  25.6 1.5 gather_fusion
  27.1 1.4 fusion.34
  31.3 1.5 gather_fusion
  32.8 1.4 fusion.34
  36.9 1.5 gather_fusion
  38.4 1.4 fusion.34
  42.5 1.5 gather_fusion
  44.0 1.4 fusion.34
  48.1 1.5 gather_fusion
  49.6 1.4 fusion.34
  54.0 22.1 %scatter_custom_fusion.3 = f32[2048]{0:T(1024)S(1)} fusion(s32[4096]{0:T(1024)S(1)} %copy-done.4, f32[4096]{0:T(1024)S(1)} %copy-done.2, f32[]{:T(128)} %constant.36.clone.1), kind=kCustom, calls=%fused_computation.37 | custom fusion | flops 4096 | bytes 8196 | tf_op jit(solution)/shard_map/scatter-add | solution.py:49
  76.1 299.0 %all-reduce.3.cloned.1.call-done = f32[131072]{0:T(1024)} async-done(((f32[131072]{0:T(1024)}), f32[131072]{0:T(1024)}) %all-reduce.3.cloned.1.call-update) | async-done | bytes 524304 | tf_op jit(solution)/shard_map/psum | solution.py:43
  375.9 22.1 %scatter_custom_fusion.2 = f32[2048]{0:T(1024)S(1)} fusion(s32[4096]{0:T(1024)S(1)} %copy-done.4, f32[4096]{0:T(1024)S(1)} %fusion.17, f32[]{:T(128)} %constant.36.clone.1), kind=kCustom, calls=%fused_computation.39 | custom fusion | flops 4096 | bytes 8196 | tf_op jit(solution)/shard_map/scatter-add | solution.py:48
  398.0 88.2 %all-reduce = (f32[2048]{0:T(1024)S(1)}, f32[2048]{0:T(1024)S(1)}) all-reduce(f32[2048]{0:T(1024)S(1)} %scatter_custom_fusion.2, f32[2048]{0:T(1024)S(1)} %scatter_custom_fusion.3), channel_id=1, replica_groups=mesh['events'=8,'shells'=32] {'events','shells'}, use_global_device_ids=true, to_apply=%region_5.6 | all-reduce | flops 4096 | bytes 32768 | tf_op jit(solution)/shard_map/psum | solution.py:50
  486.2 23.0 %gather_fusion.2 = f32[4096]{0:T(1024)S(1)} fusion(f32[2048]{0:T(1024)S(1)} %add_divide_fusion, s32[4096]{0:T(1024)S(1)} %fusion.16), kind=kCustom, calls=%fused_computation.2 | custom fusion | bytes 49152 | tf_op jit(solution)/shard_map/gather | solution.py:52
  509.2 1.3 fusion.22
  510.6 37.3 %all_gather.6 = bf16[131072]{0:T(1024)(128)(2,1)S(1)} all-gather(bf16[4096]{0:T(1024)(128)(2,1)S(1)} %get-tuple-element.125), channel_id=1, replica_groups=mesh['events'=8,'shells'=32] {'shells'}, dimensions={0}, use_global_device_ids=true | all-gather | bytes 270336 | tf_op jit(solution)/shard_map/all_gather | solution.py:54
  548.1 34.4 %while.21 = (s32[]{:T(128)}, f32[512,128]{1,0:T(8,128)S(1)}, s32[]{:T(128)}, s32[512]{0:T(512)}, s32[]{:T(128)}, /*index=5*/bf16[512,64,128]{2,1,0:T(8,128)(2,1)...) while((s32[]{:T(128)}, f32[512,128]{1,0:T(8,128)S(1)}, ...), condition=%wide.region_10.11_spmd, body=%wide.region_8.10_spmd.sunk | while | flops 533766 | bytes 837087 | solution.py:66
  549.5 1.3 fusion.38
  562.4 1.3 fusion.38
  566.7 1.3 fusion.38
  571.0 1.3 fusion.38
  575.3 1.3 fusion.38
  583.2 86.1 %all-gather.3.cloned.1.call-done = f32[8,1,65536]{2,1,0:T(1,128)} async-done(((f32[1,1,65536]{2,1,0:T(1,128)}), f32[8,1,65536]{2,1,0:T(1,128)}) %all-gather.3.cloned.1.call-update) | async-done | bytes 2097168 | tf_op jit(solution)/shard_map/all_gather | solution.py:67
  669.2 3.8 reduce_sum.9
  (96 shorter events, 51.9 us)
Async XLA Ops:
  7.2 46.8 %copy-start.2 = (f32[4096]{0:T(1024)S(1)}, f32[4096]{0:T(1024)}, u32[]{:S(2)}) copy-start(f32[4096]{0:T(1024)} %param.18) | copy-start | bytes 49156
  7.2 46.8 %copy-start.4 = (s32[4096]{0:T(1024)S(1)}, s32[4096]{0:T(1024)}, u32[]{:S(2)}) copy-start(s32[4096]{0:T(1024)} %param.19) | copy-start | bytes 49156
  7.2 368.0 %copy-start.3 = (f32[4096]{0:T(1024)S(1)}, f32[4096]{0:T(1024)}, u32[]{:S(2)}) copy-start(f32[4096]{0:T(1024)} %param.17) | copy-start | bytes 49156
  7.2 368.0 %all-reduce.3.cloned.1.call-start = ((), (), s32[]{:S(2)}) async-start(), calls=%async_computation | async-start | bytes 1048576 | tf_op jit(solution)/shard_map/psum | solution.py:43
  54.0 615.3 %all-gather.3.cloned.1.call-start = ((), (), s32[]{:S(2)}) async-start(), calls=%async_computation.1 | async-start | bytes 2359296 | tf_op jit(solution)/shard_map/all_gather | solution.py:67
  486.2 23.0 %copy-start = (f32[2048]{0:T(1024)}, f32[2048]{0:T(1024)S(1)}, u32[]{:S(2)}) copy-start(f32[2048]{0:T(1024)S(1)} %add_divide_fusion) | copy-start | bytes 24580
  582.5 0.7 copy-start.1
Sparse Core Ops, SparseCore 0:
  54.1 321.0 all-reduce.2
  583.3 85.8 all-gather.2
